TPU v7x, 32 devices: a whole 2x2x4 slice. The times are simulated.
32 devices in a mesh: grp: 2 (over y), blk: 4 (over z), tile: 4 (over x, core).
Axes of the slice: x: 2, y: 2, z: 4, core: 2. Of those that a mesh axis runs over, the one named last changes fastest.
Arguments:
- fp_values: bfloat16 [6144, 128], P(('grp', 'blk', 'tile')), parts along dimension 0, may hold values from -0.625 to 0.625
- block_owner: int32 [6144], P(('grp', 'blk', 'tile')), parts along dimension 0, may hold values from 0 to 3, as said below
- block_obs: int32 [6144], P(('grp', 'blk', 'tile')), parts along dimension 0, may hold values from 0 to 127
- block_base: int32 [6144], P(('grp', 'blk', 'tile')), parts along dimension 0, may hold values from 0 to 64
- block_count: int32 [6144], P(('grp', 'blk', 'tile')), parts along dimension 0, may hold values from 32 to 128, as said below
- cover_index: int32 [2, 128], replicated, may hold values from 0 to 191
- cover_weight: float32 [2, 128], replicated, may hold values from 0.25 to 1
- spatial_cov: bfloat16 [2048, 1024], P(('grp', 'blk'), 'tile'), parts along dimension 0, as said below
- temporal_cov: float32 [104, 52], P('grp'), parts along dimension 0, as said below
- obs_week: int32 [1024], P('grp'), parts along dimension 0, may hold values from 0 to 51
- obs_error: float32 [1024], P(('grp', 'blk')), parts along dimension 0, may hold values from 0.2 to 1
Outputs:
- panel: float32 [1024, 128], P(('grp', 'blk')), parts along dimension 0
- trailing: float32 [1024, 512], P(('grp', 'blk'), 'tile'), parts along dimension 0
There are 2 independent parts, one for each index of `grp`. A program takes and returns all parts, laid end to end along the dimension named above; an argument that names none is the same for every part. Nothing has to cross between parts.
Inputs may be any that keep to these rules, and one draw needn't show every extreme that they name: `block_owner`: no tile is named by more than 64 of one device's 192 blocks; in every observation block one tile is named by exactly 64 blocks of each of its devices. `block_count`: each device holds at least one block with all cells valid. `spatial_cov`: symmetric positive definite. `temporal_cov`: symmetric positive definite.
All inputs are finite; a program needn't handle non-finite values.
Results may differ from a plain program's by a relative error of at most 0.0033.
Values may be sent and summed in bfloat16 or wider, within the bound.
No kernel may reach another device: no remote copies, remote signals or barrier semaphores. Data moves between devices by JAX's collectives and lax.ppermute only.
A program may use at most 64 MiB of HBM per device.

v0:
```python
import jax
import jax.numpy as jnp
from jax import lax
from jax.sharding import PartitionSpec as P

PANEL_MAX = 128


def broadcast(value, axis, root):
    mine = lax.axis_index(axis) == root
    return lax.psum(jnp.where(mine, value, jnp.zeros_like(value)), axis)


def kept_values(fp_values, block_count):
    keep_mask = lax.broadcasted_iota(jnp.int32, fp_values.shape, 1) < block_count[:, None]
    return jnp.where(keep_mask, fp_values, jnp.zeros_like(fp_values))


def regrid(values, rows, offsets, cover_index, cover_weight, out_rows, out_cols):
    contrib = values.astype(jnp.float32)[:, None, :] * cover_weight[None, :, :]
    columns = offsets[:, None, None] + cover_index[None, :, :]
    row_index = jnp.broadcast_to(rows[:, None, None], columns.shape)
    return jnp.zeros((out_rows, out_cols), jnp.float32).at[row_index, columns].add(contrib)


def top_rows(local, rank):
    return jnp.where(rank == 0, local, jnp.zeros_like(local))


def contract_last(left, right):
    return lax.dot_general(
        left, right, (((1,), (1,)), ((), ())), preferred_element_type=jnp.float32
    )


def body(
    fp_values,
    block_owner,
    block_obs,
    block_base,
    block_count,
    cover_index,
    cover_weight,
    spatial_cov,
    temporal_cov,
    obs_week,
    obs_error,
):
    n_tile = lax.axis_size("tile")
    n_blk = lax.axis_size("blk")
    tile_rank = lax.axis_index("tile")
    blk_rank = lax.axis_index("blk")
    cell_tile = spatial_cov.shape[1]
    obs_rows = obs_error.shape[0]
    all_cells = cell_tile * n_tile
    col_count = obs_rows * n_blk // n_tile
    panel_width = min(PANEL_MAX, col_count)
    kept = kept_values(fp_values, block_count)
    dense = regrid(
        kept,
        block_obs,
        block_owner * cell_tile + block_base,
        cover_index,
        cover_weight,
        obs_rows,
        all_cells,
    )
    tile_sum = lax.psum_scatter(dense, "tile", scatter_dimension=1, tiled=True)
    footprints = tile_sum.astype(jnp.bfloat16)
    row_prints = lax.all_gather(footprints, "tile", axis=1, tiled=True)
    product = jnp.dot(
        row_prints,
        lax.all_gather(spatial_cov, "blk", axis=0, tiled=True),
        preferred_element_type=jnp.float32,
    ).astype(jnp.bfloat16)
    terms = contract_last(product, lax.all_gather(footprints, "blk", axis=0, tiled=True))
    pairs = lax.psum_scatter(terms, "tile", scatter_dimension=1, tiled=True)
    week_count = temporal_cov.shape[0]
    week_ids = jnp.arange(week_count, dtype=jnp.int32)
    row_weeks = lax.dynamic_slice_in_dim(obs_week, blk_rank * obs_rows, obs_rows)
    col_weeks = lax.dynamic_slice_in_dim(obs_week, tile_rank * col_count, col_count)
    row_onehot = (row_weeks[:, None] == week_ids[None, :]).astype(jnp.float32)
    col_onehot = (col_weeks[:, None] == week_ids[None, :]).astype(jnp.float32)
    row_cov = jnp.dot(row_onehot, temporal_cov, precision=lax.Precision.HIGHEST)
    week_cov = lax.dot_general(
        row_cov, col_onehot, (((1,), (1,)), ((), ())), precision=lax.Precision.HIGHEST
    )
    row_global = blk_rank * obs_rows + jnp.arange(obs_rows, dtype=jnp.int32)
    col_global = tile_rank * col_count + jnp.arange(col_count, dtype=jnp.int32)
    diagonal = jnp.where(row_global[:, None] == col_global[None, :], obs_error[:, None], 0.0)
    innovation = pairs * week_cov + diagonal
    panel_columns = broadcast(innovation[:, :panel_width], "tile", 0)
    top_group, top_left = lax.psum(
        (top_rows(innovation, blk_rank), top_rows(panel_columns, blk_rank)), "blk"
    )
    pivot = jnp.linalg.cholesky(0.5 * (top_left + top_left.T))
    panel = jax.scipy.linalg.solve_triangular(pivot, panel_columns.T, lower=True).T
    column_factor = jax.scipy.linalg.solve_triangular(pivot, top_group, lower=True).T
    trailing = innovation - jnp.dot(panel, column_factor.T, precision=lax.Precision.HIGHEST)
    return (panel, trailing)


def solution(mesh):
    placed = (
        P(("grp", "blk", "tile"), None),
        P(("grp", "blk", "tile")),
        P(("grp", "blk", "tile")),
        P(("grp", "blk", "tile")),
        P(("grp", "blk", "tile")),
        P(),
        P(),
        P(("grp", "blk"), "tile"),
        P("grp", None),
        P("grp"),
        P(("grp", "blk")),
    )
    return jax.shard_map(
        body,
        mesh=mesh,
        in_specs=placed,
        out_specs=(P(("grp", "blk"), None), P(("grp", "blk"), "tile")),
        check_vma=False,
    )
```

profile of v0, /device:TPU:0, one launch (start us, length us, event | category | flops | bytes accessed | tf_op | source)
XLA Modules:
  0.0 524.8 jit_solution(15512923887324170173)
XLA Ops:
  7.2 0.0 reduce-scatter.3.cloned.1.call-start
  7.2 0.7 broadcast_add_fusion
  8.0 0.7 copy-done.10
  8.6 0.7 copy-done.7
  9.3 0.2 compare_select_fusion
  9.5 0.6 copy-done.14
  10.1 0.1 and_reduce_fusion
  10.3 0.5 copy-done.15
  10.8 0.1 multiply_reduce_fusion
  10.9 0.2 copy.22
  11.1 0.6 copy-done.5
  11.7 0.1 fusion.14
  11.8 0.6 copy-done.9
  12.4 0.1 broadcast_multiply_fusion
  12.5 339.3 %scatter_custom_fusion = f32[131072]{0:T(1024)S(1)} fusion(s32[49152]{0:T(1024)S(1)} %bitcast.32, f32[49152]{0:T(1024)S(1)} %bitcast.33, f32[]{:T(128)} %constant.58.clone.1), kind=kCustom, calls=%fused_computation.10 | custom fusion | flops 49152 | bytes 524292
  351.8 0.9 reshape.48
  352.7 0.0 reduce-scatter.3.cloned.1.call-update
  352.7 0.0 reduce-scatter.5.cloned.1.call-start
  352.8 0.8 copy-done.3
  353.6 17.4 %all_gather.10 = bf16[1024,256]{1,0:T(8,128)(2,1)S(1)} all-gather(bf16[256,256]{1,0:T(8,128)(2,1)S(1)} %copy-done.3), channel_id=1, replica_groups=mesh['grp'=2,'blk'=4,'tile'=4] {'blk'}, dimensions={0}, use_global_device_ids=true | all-gather | bytes 655360 | tf_op jit(solution)/shard_map/all_gather | solution.py:73
  371.0 6.3 %reduce-scatter.3.cloned.1.call-done = f32[128,256]{1,0:T(8,128)} async-done(((f32[128,1024]{1,0:T(8,128)}), f32[128,256]{1,0:T(8,128)}) %reduce-scatter.3.cloned.1.call-update) | async-done | bytes 131088 | tf_op jit(solution)/shard_map/reduce_scatter | solution.py:68
  377.3 0.9 convert_element_type.12
  378.2 13.8 %all_gather.11 = bf16[512,256]{1,0:T(8,128)(2,1)S(1)} all-gather(bf16[128,256]{1,0:T(8,128)(2,1)S(1)} %convert_element_type.12), channel_id=1, replica_groups=mesh['grp'=2,'blk'=4,'tile'=4] {'blk'}, dimensions={0}, use_global_device_ids=true | all-gather | bytes 327680 | tf_op jit(solution)/shard_map/all_gather | solution.py:76
  392.0 5.8 %all_gather.9 = bf16[128,1024]{1,0:T(8,128)(2,1)S(1)} all-gather(bf16[128,256]{1,0:T(8,128)(2,1)S(1)} %convert_element_type.12), channel_id=1, replica_groups=mesh['grp'=2,'blk'=4,'tile'=4] {'tile'}, dimensions={1}, use_global_device_ids=true | all-gather | bytes 327680 | tf_op jit(solution)/shard_map/all_gather | solution.py:70
  397.7 1.2 fusion
  398.9 0.0 reduce-scatter.5.cloned.1.call-update
  398.9 0.0 all-reduce.4.cloned.1.call-start
  399.0 0.7 copy-done.13
  399.7 0.1 fusion.17
  399.8 0.3 fusion.13
  400.1 19.8 %reduce-scatter.5.cloned.1.call-done = f32[128,128]{1,0:T(8,128)} async-done(((f32[128,512]{1,0:T(8,128)}), f32[128,128]{1,0:T(8,128)}) %reduce-scatter.5.cloned.1.call-update) | async-done | bytes 65552 | tf_op jit(solution)/shard_map/reduce_scatter | solution.py:77
  419.9 0.7 copy-done.12
  420.5 1.8 broadcast_select_fusion.2
  422.3 0.0 all-reduce.6.cloned.1.call-start
  422.4 31.9 %all-reduce.4.cloned.1.call-done = f32[128,128]{1,0:T(8,128)} async-done(((f32[128,128]{1,0:T(8,128)}), f32[128,128]{1,0:T(8,128)}) %all-reduce.4.cloned.1.call-update) | async-done | bytes 65552 | tf_op jit(solution)/shard_map/psum | solution.py:11
  454.3 1.5 broadcast_select_fusion.3
  455.8 36.0 %all-reduce.6.cloned.1.call-done = (f32[128,128]{1,0:T(8,128)}, f32[128,128]{1,0:T(8,128)}) async-done(((f32[128,128]{1,0:T(8,128)}, f32[128,128]{1,0:T(8,128)}), (f32[128,128]{1,0:T(8,128)}, f32[128,128]{1,0:T(8,128)})) %all-reduce.6.cloned.1.call-update) | async-done | bytes 131088 | tf_op jit(solution)/shard_map/psum | solution.py:93
  491.8 1.0 copy.23
  492.9 0.1 copy.24
  493.0 11.7 %cholesky.17 = f32[128,128]{1,0:T(8,128)S(1)} custom-call(f32[128,128]{1,0:T(8,128)S(1)} %fusion.11), custom_call_target="Cholesky" | custom-call | tf_op jit(solution)/shard_map/jit(cholesky)/cholesky | solution.py:96
  504.7 0.6 compare_reduce_fusion
  505.4 0.7 fusion.5
  506.1 9.8 %custom-call.7 = f32[1,128,128]{1,2,0:T(8,128)S(1)} custom-call(f32[1,128,128]{2,1,0:T(8,128)S(1)} %fusion.5), custom_call_target="InvertDiagBlocksLowerTriangular" | custom-call | tf_op jit(solution)/shard_map/jit(_solve_triangular)/triangular_solve | solution.py:97
  515.9 0.3 fusion.6
  516.2 0.7 copy.25
  516.9 0.1 copy-done.4
  517.0 0.3 fusion.8
  517.3 0.9 convolution_subtract_fusion
  (31 shorter events, 0.2 us)
Async XLA Ops:
  7.2 392.6 %copy-start = (f32[52,52]{1,0:T(8,128)S(1)}, f32[52,52]{1,0:T(8,128)}, u32[]{:S(2)}) copy-start(f32[52,52]{1,0:T(8,128)} %param.21) | copy-start | bytes 32452
  7.2 0.8 copy-start.6
  7.2 370.1 %reduce-scatter.3.cloned.1.call-start = ((), (), s32[]{:S(2)}) async-start(), calls=%async_computation.2 | async-start | bytes 655360 | tf_op jit(solution)/shard_map/reduce_scatter | solution.py:68
  7.2 0.7 copy-start.11
  7.9 0.7 copy-start.10
  8.6 0.7 copy-start.7
  9.5 0.7 copy-start.14
  10.1 0.7 copy-start.15
  10.9 0.8 copy-start.5
  10.9 0.8 copy-start.8
  11.7 0.7 copy-start.9
  352.7 0.9 copy-start.3
  352.7 67.2 %reduce-scatter.5.cloned.1.call-start = ((), (), s32[]{:S(2)}) async-start(), calls=%async_computation.3 | async-start | bytes 327680 | tf_op jit(solution)/shard_map/reduce_scatter | solution.py:77
  398.9 55.4 %all-reduce.4.cloned.1.call-start = ((), (), s32[]{:S(2)}) async-start(), calls=%async_computation.4 | async-start | bytes 131072 | tf_op jit(solution)/shard_map/psum | solution.py:11
  399.0 0.7 copy-start.13
  419.9 0.7 copy-start.12
  422.3 69.5 %all-reduce.6.cloned.1.call-start = ((), (), s32[]{:S(2)}) async-start(), calls=%async_computation.5 | async-start | bytes 262144 | tf_op jit(solution)/shard_map/psum | solution.py:93
  491.8 1.0 copy-start.2
  505.4 10.5 %copy-start.1 = (f32[128,128]{1,0:T(8,128)S(1)}, f32[128,128]{1,0:T(8,128)}, u32[]{:S(2)}) copy-start(f32[128,128]{1,0:T(8,128)} %all-reduce.4.cloned.1.call-done) | copy-start | bytes 196612
  516.2 0.8 copy-start.4
Sparse Core Ops, SparseCore 0:
  352.8 24.3 reduce-scatter.2
  399.1 20.7 reduce-scatter.4
  422.8 31.5 all-reduce.3
  457.1 34.6 all-reduce.5
where the time goes:
time: 525 us
  other arithmetic  366 us (70%)
  waiting for transfers between devices  94.1 us (18%)
  blocking collectives  36.9 us (7%)
  between operations  14 us (3%)
  local copies, waits for them, and re-layouts  8.9 us (2%)
    unnamed x4, other arithmetic  340 us
    psum x1, waiting for transfers between devices, body(): lax.psum((top_rows(innovation, blk_rank), top_rows(panel_columns, blk_ran...  36 us
    psum x1, waiting for transfers between devices, broadcast(): return lax.psum(jnp.where(mine, value, jnp.zeros_like(value)), axis)  31.9 us
    reduce_scatter x1, waiting for transfers between devices, body(): pairs = lax.psum_scatter(terms, 'tile', scatter_dimension=1, tiled=True)  19.8 us
    all_gather x1, blocking collectives, body(): lax.all_gather(spatial_cov, 'blk', axis=0, tiled=True)  17.4 us
    all_gather x1, blocking collectives, body(): lax.all_gather(footprints, 'blk', axis=0, tiled=True)  13.8 us
    another operation x3, other arithmetic, body(): pivot = jnp.linalg.cholesky(0.5 * (top_left + top_left.T))  12.4 us
  transfers between devices with their start and end apart: 4, of which 4 were waited for; matrix products, arithmetic and copies ran while one was open for 0% of the time, Pallas kernels for 0%

commit v1 on v0

--- a/solution.py
+++ b/solution.py
@@ -8,7 +8,7 @@
 
 def broadcast(value, axis, root):
     mine = lax.axis_index(axis) == root
-    return lax.psum(jnp.where(mine, value, jnp.zeros_like(value)), axis)
+    return jnp.sum(lax.all_gather(jnp.where(mine, value, jnp.zeros_like(value)), axis), axis=0)
 
 
 def kept_values(fp_values, block_count):

time: 525 us -> 497 us (0.947)
  waiting for transfers between devices: 94.1 us -> 61 us
  blocking collectives: 36.9 us -> 42.7 us
    psum x1 -> x0, waiting for transfers between devices: 31.9 us -> none  [broadcast(): return lax.psum(jnp.where(mine, value, jnp.zeros_like(value)), axis)]
    all_gather x0 -> x1, blocking collectives: none -> 5.76 us  [broadcast(): lax.all_gather(jnp.where(mine, value, jnp.zeros_like(value)), axis)]
  transfers between devices with their start and end apart: 4 -> 3, of which waited for: 4 -> 3; matrix products, arithmetic and copies ran while one was open for 0% -> 0% of each run, Pallas kernels for 0% -> 0%
where the time goes in v1:
time: 497 us; the launch traced here: 496 us
  other arithmetic  365 us (73%)
  waiting for transfers between devices  61 us (12%)
  blocking collectives  42.7 us (9%)
  between operations  14 us (3%)
  local copies, waits for them, and re-layouts  8.9 us (2%)
    unnamed x4, other arithmetic  340 us
    psum x1, waiting for transfers between devices, body(): lax.psum((top_rows(innovation, blk_rank), top_rows(panel_columns, blk_ran...  34.9 us
    reduce_scatter x1, waiting for transfers between devices, body(): pairs = lax.psum_scatter(terms, 'tile', scatter_dimension=1, tiled=True)  19.8 us
    all_gather x1, blocking collectives, body(): lax.all_gather(spatial_cov, 'blk', axis=0, tiled=True)  17.4 us
    all_gather x1, blocking collectives, body(): lax.all_gather(footprints, 'blk', axis=0, tiled=True)  13.8 us
    another operation x3, other arithmetic, body(): pivot = jnp.linalg.cholesky(0.5 * (top_left + top_left.T))  12.4 us
    another operation x2, other arithmetic, body(): jax.scipy.linalg.solve_triangular(pivot, panel_columns.T, lower=True)  10.5 us
  transfers between devices with their start and end apart: 3, of which 3 were waited for; matrix products, arithmetic and copies ran while one was open for 0% of the time, Pallas kernels for 0%

profile of v1, /device:TPU:0, one launch (start us, length us, event | category | flops | bytes accessed | tf_op | source)
XLA Modules:
  0.0 496.5 jit_solution(4993028759853959987)
XLA Ops:
  7.2 0.0 reduce-scatter.3.cloned.1.call-start
  7.2 0.7 broadcast_add_fusion
  8.0 0.7 copy-done.9
  8.6 0.7 copy-done.6
  9.3 0.2 compare_select_fusion
  9.5 0.6 copy-done.13
  10.1 0.1 and_reduce_fusion
  10.3 0.5 copy-done.14
  10.8 0.1 multiply_reduce_fusion
  10.9 0.2 copy.22
  11.1 0.6 copy-done.4
  11.7 0.1 fusion.14
  11.8 0.6 copy-done.8
  12.4 0.1 broadcast_multiply_fusion
  12.5 339.3 %scatter_custom_fusion = f32[131072]{0:T(1024)S(1)} fusion(s32[49152]{0:T(1024)S(1)} %bitcast.34, f32[49152]{0:T(1024)S(1)} %bitcast.35, f32[]{:T(128)} %constant.58.clone.1), kind=kCustom, calls=%fused_computation.10 | custom fusion | flops 49152 | bytes 524292
  351.8 0.9 reshape.48
  352.7 0.0 reduce-scatter.3.cloned.1.call-update
  352.7 0.0 reduce-scatter.5.cloned.1.call-start
  352.8 0.8 copy-done.2
  353.6 17.4 %all_gather.16 = bf16[1024,256]{1,0:T(8,128)(2,1)S(1)} all-gather(bf16[256,256]{1,0:T(8,128)(2,1)S(1)} %copy-done.2), channel_id=1, replica_groups=mesh['grp'=2,'blk'=4,'tile'=4] {'blk'}, dimensions={0}, use_global_device_ids=true | all-gather | bytes 655360 | tf_op jit(solution)/shard_map/all_gather | solution.py:73
  371.0 6.3 %reduce-scatter.3.cloned.1.call-done = f32[128,256]{1,0:T(8,128)} async-done(((f32[128,1024]{1,0:T(8,128)}), f32[128,256]{1,0:T(8,128)}) %reduce-scatter.3.cloned.1.call-update) | async-done | bytes 131088 | tf_op jit(solution)/shard_map/reduce_scatter | solution.py:68
  377.2 0.9 convert_element_type.12
  378.2 13.8 %all_gather.17 = bf16[512,256]{1,0:T(8,128)(2,1)S(1)} all-gather(bf16[128,256]{1,0:T(8,128)(2,1)S(1)} %convert_element_type.12), channel_id=1, replica_groups=mesh['grp'=2,'blk'=4,'tile'=4] {'blk'}, dimensions={0}, use_global_device_ids=true | all-gather | bytes 327680 | tf_op jit(solution)/shard_map/all_gather | solution.py:76
  392.0 5.8 %all_gather.15 = bf16[128,1024]{1,0:T(8,128)(2,1)S(1)} all-gather(bf16[128,256]{1,0:T(8,128)(2,1)S(1)} %convert_element_type.12), channel_id=1, replica_groups=mesh['grp'=2,'blk'=4,'tile'=4] {'tile'}, dimensions={1}, use_global_device_ids=true | all-gather | bytes 327680 | tf_op jit(solution)/shard_map/all_gather | solution.py:70
  397.7 1.2 fusion
  398.9 0.0 reduce-scatter.5.cloned.1.call-update
  398.9 0.0 all-reduce.3.cloned.1.call-start
  399.0 0.7 copy-done.12
  399.7 0.1 fusion.17
  399.8 0.3 fusion.13
  400.0 19.8 %reduce-scatter.5.cloned.1.call-done = f32[128,128]{1,0:T(8,128)} async-done(((f32[128,512]{1,0:T(8,128)}), f32[128,128]{1,0:T(8,128)}) %reduce-scatter.5.cloned.1.call-update) | async-done | bytes 65552 | tf_op jit(solution)/shard_map/reduce_scatter | solution.py:77
  419.9 0.7 copy-done.11
  420.5 1.8 broadcast_select_fusion.2
  422.3 5.8 %all-gather = f32[512,128]{1,0:T(8,128)S(1)} all-gather(f32[128,128]{1,0:T(8,128)S(1)} %get-tuple-element.14), channel_id=2, replica_groups=mesh['grp'=2,'blk'=4,'tile'=4] {'tile'}, dimensions={0}, use_global_device_ids=true | all-gather | bytes 327680 | tf_op jit(solution)/shard_map/all_gather | solution.py:11
  428.1 0.6 broadcast_select_fusion.3
  428.7 0.0 all-reduce.3.cloned.1.call-update
  428.7 34.9 %all-reduce.3.cloned.1.call-done = (f32[128,128]{1,0:T(8,128)}, f32[128,128]{1,0:T(8,128)}) async-done(((f32[128,128]{1,0:T(8,128)}, f32[128,128]{1,0:T(8,128)}), (f32[128,128]{1,0:T(8,128)}, f32[128,128]{1,0:T(8,128)})) %all-reduce.3.cloned.1.call-update) | async-done | bytes 131088 | tf_op jit(solution)/shard_map/psum | solution.py:93
  463.6 1.0 copy.23
  464.6 0.1 copy.24
  464.8 11.7 %cholesky.17 = f32[128,128]{1,0:T(8,128)S(1)} custom-call(f32[128,128]{1,0:T(8,128)S(1)} %fusion.11), custom_call_target="Cholesky" | custom-call | tf_op jit(solution)/shard_map/jit(cholesky)/cholesky | solution.py:96
  476.5 0.6 compare_reduce_fusion
  477.1 0.7 fusion.5
  477.8 9.8 %custom-call.7 = f32[1,128,128]{1,2,0:T(8,128)S(1)} custom-call(f32[1,128,128]{2,1,0:T(8,128)S(1)} %fusion.5), custom_call_target="InvertDiagBlocksLowerTriangular" | custom-call | tf_op jit(solution)/shard_map/jit(_solve_triangular)/triangular_solve | solution.py:97
  487.6 0.3 fusion.6
  487.9 0.7 copy.25
  488.7 0.1 copy-done.3
  488.8 0.3 fusion.8
  489.0 0.9 convolution_subtract_fusion
  (28 shorter events, 0.2 us)
Async XLA Ops:
  7.2 392.6 %copy-start = (f32[52,52]{1,0:T(8,128)S(1)}, f32[52,52]{1,0:T(8,128)}, u32[]{:S(2)}) copy-start(f32[52,52]{1,0:T(8,128)} %param.21) | copy-start | bytes 32452
  7.2 0.8 copy-start.5
  7.2 370.1 %reduce-scatter.3.cloned.1.call-start = ((), (), s32[]{:S(2)}) async-start(), calls=%async_computation.2 | async-start | bytes 655360 | tf_op jit(solution)/shard_map/reduce_scatter | solution.py:68
  7.2 0.7 copy-start.10
  7.9 0.7 copy-start.9
  8.6 0.7 copy-start.6
  9.5 0.7 copy-start.13
  10.1 0.7 copy-start.14
  10.9 0.8 copy-start.4
  10.9 0.8 copy-start.7
  11.7 0.7 copy-start.8
  352.7 0.9 copy-start.2
  352.7 67.2 %reduce-scatter.5.cloned.1.call-start = ((), (), s32[]{:S(2)}) async-start(), calls=%async_computation.3 | async-start | bytes 327680 | tf_op jit(solution)/shard_map/reduce_scatter | solution.py:77
  398.9 64.7 %all-reduce.3.cloned.1.call-start = ((), (), s32[]{:S(2)}) async-start(), calls=%async_computation.4 | async-start | bytes 262144 | tf_op jit(solution)/shard_map/psum | solution.py:93
  399.0 0.7 copy-start.12
  419.9 0.7 copy-start.11
  463.6 1.0 copy-start.1
  487.9 0.8 copy-start.3
Sparse Core Ops, SparseCore 0:
  352.8 24.3 reduce-scatter.2
  399.1 20.7 reduce-scatter.4
  428.9 34.6 all-reduce.2
